TPU v7x, 32 devices: a whole 2x2x4 slice. The times are simulated.
32 devices in a mesh: segment: 4 (over y, x), col: 8 (over z, core).
Axes of the slice: x: 2, y: 2, z: 4, core: 2. Of those that a mesh axis runs over, the one named last changes fastest.
Arguments:
- left_env: bfloat16 [384, 8192], P(None, 'col'), may hold values from -6 to 6
- bit_strings: int32 [384, 4], P(None, 'segment'), may hold values from 0 to 1
- site_tensors: bfloat16 [4, 2, 8192, 8192], P('segment', None, None, 'col'), may hold values from -0.0625 to 0.0625
Outputs:
- section_env: bfloat16 [4, 384, 8192], P('segment', None, 'col')
- section_log: float32 [4, 384], P('segment')
All inputs are finite; a program needn't handle non-finite values. Where the computation divides by a largest or mean magnitude, that divisor is 1e-20 or more.
Results may differ from a plain program's by a relative error of at most 0.0065.
Values may be sent and summed in bfloat16 or wider, within the bound.
A program may use at most 128 MiB of HBM per device.

v0:
```python
import functools

import jax
import jax.numpy as jnp
from jax import lax
from jax.experimental import pallas as pl
from jax.experimental.pallas import tpu as pltpu
from jax.sharding import PartitionSpec as P

GRANULES = 8
DIRECT = True
EPSILON = 1e-06
MESH = pl.DeviceIdType.MESH


def granules_of(rows):
    for count in range(GRANULES, 0, -1):
        if rows % count == 0 and (rows // count) % 16 == 0:
            return count
    return 1


def chip_at(step, z, n):
    below, above = z, n - 1 - z
    both = jnp.minimum(below, above)
    paired = (step + 1) // 2
    near = jnp.where(step % 2 == 1, z - paired, z + paired)
    far = jnp.where(below < above, z + (step - both), z - (step - both))
    return jnp.where(step <= 2 * both, near, far)


def kernel(
    stages, peers, granules,
    env_in, bits_in, tensor_in, env_out, log_out,
    weights, pieces, product, outgoing, peak, peak_sent, peak_all, scale_in, scale_sent,
    load_sem, weight_sem, arrive_sem, line_sem, cross_sem, next_sem,
    peak_send_sem, peak_recv_sem, scale_send_sem, scale_recv_sem,
):
    rows, width = outgoing.shape
    block = rows // granules
    n = peers // 2
    stage = lax.axis_index("segment")
    me = lax.axis_index("col")
    z = me // 2
    core = me % 2

    def there(segment, col):
        return {"segment": segment, "col": col}

    load = pltpu.make_async_copy(env_in, pieces.at[me], load_sem)

    @pl.when(stage == 0)
    def _():
        load.start()

    def owner_at(step):
        chip = chip_at(step % n, z, n)
        return chip, chip * 2 + jnp.where(step < n, core, 1 - core)

    def weight_copy(owner):
        return pltpu.make_async_copy(
            tensor_in.at[0, :, pl.ds(pl.multiple_of(owner * width, width), width), :],
            weights.at[owner],
            weight_sem.at[owner],
        )

    def start_weight(step, carry):
        weight_copy(owner_at(step)[1]).start()
        return carry

    lax.fori_loop(0, peers, start_weight, 0)

    barrier = pltpu.get_barrier_semaphore()

    def greet(by, carry):
        pl.semaphore_signal(
            barrier, inc=1, device_id=there(stage, (me + by) % peers), device_id_type=MESH
        )
        return carry

    lax.fori_loop(1, peers, greet, 0)

    count = jnp.int32(0)
    for by in (-2, -1, 0, 1, 2):
        inside = (z + by >= 0) & (z + by < n)
        for other in (-1, 1):
            meets = inside & (stage + other >= 0) & (stage + other < stages)

            @pl.when(meets)
            def _():
                pl.semaphore_signal(
                    barrier,
                    inc=1,
                    device_id=there(stage + other, me + 2 * by),
                    device_id_type=MESH,
                )

            count = count + jnp.where(meets, 1, 0)
    pl.semaphore_wait(barrier, peers - 1 + count)

    @pl.when(stage == 0)
    def _():
        load.wait()

    def rows_of(granule):
        return pl.ds(pl.multiple_of(granule * block, block), block)

    def piece(granule, owner):
        return pieces.at[owner, rows_of(granule), :]

    def send(source, granule, owner, sem, segment, col):
        return pltpu.make_async_remote_copy(
            src_ref=source,
            dst_ref=piece(granule, owner),
            send_sem=sem,
            recv_sem=arrive_sem.at[granule, owner],
            device_id=there(segment, col),
            device_id_type=MESH,
        )

    def cross(granule, owner):
        col = 2 * z + 1 - core
        return send(
            piece(granule, owner), granule, owner, cross_sem.at[granule, owner // 2], stage, col
        )

    def along(act, granule, chip):
        owner = chip * 2 + core
        source = piece(granule, owner)
        for slot, by in enumerate((1, -1, 2, -2)):
            ahead = chip <= z if by > 0 else chip >= z
            if DIRECT:
                ahead = ahead & ((chip != z) | (stage == 0))

            @pl.when(ahead & ((z - chip) % 2 == 0) & (z + by >= 0) & (z + by < n))
            def _():
                sem = line_sem.at[slot, granule, chip]
                act(send(source, granule, owner, sem, stage, me + 2 * by))

    def onward(act, granule):
        source = outgoing.at[rows_of(granule), :]
        for slot, by in enumerate((0, 1, -1, 2, -2) if DIRECT else (0,)):

            @pl.when((stage < stages - 1) & (z + by >= 0) & (z + by < n))
            def _():
                sem = next_sem.at[slot, granule]
                act(send(source, granule, me, sem, stage + 1, me + 2 * by))

    def start(copy):
        copy.start()

    def sent(copy):
        copy.wait_send()

    def open_granule(granule):
        @pl.when(stage == 0)
        def _():
            along(start, granule, z)
            cross(granule, me).start()

    open_granule(0)

    def one_granule(granule, carry):
        @pl.when(granule + 1 < granules)
        def _():
            open_granule(granule + 1)

        bit = bits_in[rows_of(granule), :].astype(jnp.float32).astype(jnp.bfloat16)

        def one_piece(step, carry):
            chip, owner = owner_at(step)

            @pl.when((stage > 0) | (step > 0))
            def _():
                cross(granule, owner).wait_recv()

                @pl.when(step < n)
                def _():
                    along(start, granule, chip)
                    cross(granule, owner).start()

            @pl.when(granule == 0)
            def _():
                weight_copy(owner).wait()

            value = piece(granule, owner)[...]
            one = value * bit
            both = jnp.concatenate([value - one, one], axis=1)
            part = jnp.dot(
                both,
                weights[owner].reshape(2 * width, width),
                preferred_element_type=jnp.float32,
            )

            @pl.when(step == 0)
            def _():
                product[rows_of(granule), :] = part

            @pl.when(step > 0)
            def _():
                product[rows_of(granule), :] += part

            return carry

        lax.fori_loop(0, peers, one_piece, 0)
        done = product[rows_of(granule), :]
        outgoing[rows_of(granule), :] = done.astype(jnp.bfloat16)

        onward(start, granule)

        largest = jnp.max(jnp.abs(done), axis=1, keepdims=True)
        peak[rows_of(granule), :] = jnp.broadcast_to(largest, (block, peak.shape[1]))
        return carry

    lax.fori_loop(0, granules, one_granule, 0)

    mine = jnp.transpose(peak[...])[:8]
    peak_sent[...] = mine

    def peak_copy(by):
        return pltpu.make_async_remote_copy(
            src_ref=peak_sent,
            dst_ref=peak_all.at[by],
            send_sem=peak_send_sem.at[by],
            recv_sem=peak_recv_sem.at[by],
            device_id=there(stage, (me + by) % peers),
            device_id_type=MESH,
        )

    def start_peak(by, carry):
        peak_copy(by).start()
        return carry

    lax.fori_loop(1, peers, start_peak, 0)

    scale_copy = pltpu.make_async_remote_copy(
        src_ref=scale_sent,
        dst_ref=scale_in,
        send_sem=scale_send_sem,
        recv_sem=scale_recv_sem,
        device_id=there(stage + 1, me),
        device_id_type=MESH,
    )

    @pl.when(stage == 0)
    def _():
        scale_in[...] = jnp.ones_like(scale_in)

    @pl.when(stage > 0)
    def _():
        scale_copy.wait_recv()

    def take_peak(by, largest):
        peak_copy(by).wait_recv()
        return jnp.maximum(largest, peak_all[by])

    largest = lax.fori_loop(1, peers, take_peak, mine)
    before = scale_in[...]
    scale = largest + EPSILON * before
    scale_sent[...] = scale

    @pl.when(stage < stages - 1)
    def _():
        scale_copy.start()

    log_out[...] = jnp.log(largest / before + EPSILON)[:1]
    by_row = jnp.transpose(jnp.broadcast_to(scale[:1], (128, rows)))[:, :1]
    env_out[0] = (product[...] / by_row).astype(jnp.bfloat16)

    def drain(granule, carry):
        def drain_chip(chip, carry):
            along(sent, granule, chip)
            cross(granule, chip * 2 + core).wait_send()
            return carry

        lax.fori_loop(0, n, drain_chip, 0)
        onward(sent, granule)
        return carry

    lax.fori_loop(0, granules, drain, 0)

    def drain_peak(by, carry):
        peak_copy(by).wait_send()
        return carry

    lax.fori_loop(1, peers, drain_peak, 0)

    @pl.when(stage < stages - 1)
    def _():
        scale_copy.wait_send()


def solution(mesh):
    stages, peers = mesh.shape["segment"], mesh.shape["col"]
    n = peers // 2

    def local(left_env, bit_strings, site_tensors):
        rows, width = left_env.shape
        granules = granules_of(rows)
        vmem = pl.BlockSpec(memory_space=pltpu.VMEM)
        anywhere = pl.BlockSpec(memory_space=pl.ANY)
        dma = pltpu.SemaphoreType.DMA
        return pl.pallas_call(
            functools.partial(kernel, stages, peers, granules),
            out_shape=(
                jax.ShapeDtypeStruct((1, rows, width), jnp.bfloat16),
                jax.ShapeDtypeStruct((1, rows), jnp.float32),
            ),
            in_specs=[anywhere, vmem, anywhere],
            out_specs=(vmem, vmem),
            scratch_shapes=[
                pltpu.VMEM((peers, 2, width, width), jnp.bfloat16),
                pltpu.VMEM((peers, rows, width), jnp.bfloat16),
                pltpu.VMEM((rows, width), jnp.float32),
                pltpu.VMEM((rows, width), jnp.bfloat16),
                pltpu.VMEM((rows, 128), jnp.float32),
                pltpu.VMEM((8, rows), jnp.float32),
                pltpu.VMEM((peers, 8, rows), jnp.float32),
                pltpu.VMEM((8, rows), jnp.float32),
                pltpu.VMEM((8, rows), jnp.float32),
                dma,
                dma((peers,)),
                dma((granules, peers)),
                dma((4, granules, n)),
                dma((granules, n)),
                dma((5, granules)),
                dma((peers,)),
                dma((peers,)),
                dma,
                dma,
            ],
            compiler_params=pltpu.CompilerParams(
                collective_id=0, has_side_effects=True, vmem_limit_bytes=60 * 1024 * 1024
            ),
        )(left_env, bit_strings, site_tensors)

    return jax.shard_map(
        local,
        mesh=mesh,
        in_specs=(P(None, "col"), P(None, "segment"), P("segment", None, None, "col")),
        out_specs=(P("segment", None, "col"), P("segment", None)),
        check_vma=False,
    )
```

profile of v0, /device:TPU:7, one launch (start us, length us, event | category | flops | bytes accessed | tf_op | source)
XLA Modules:
  0.0 162.6 jit_solution(8044865299323121357)
XLA Ops:
  0.6 1.5 copy.5.bits_in
  2.1 157.1 %shard_map.50 = (bf16[1,384,1024]{2,1,0:T(8,128)(2,1)}, f32[1,384]{1,0:T(1,128)}) custom-call(bf16[384,1024]{1,0:T(8,128)(2,1)} %env_in.1, s32[384,1]{1,0:T(8,128)} %copy.5.bits_in, bf16[1,2,8192,1024]{3,2,1,0:T(8,128)(2,1)} %tensor_in.1), custom_call_target="tpu_custom_call" | custom-call | tf_op jit(solution)/shard_map/pallas_call | solution.py:303
  159.3 2.1 %copy.8 = bf16[1,384,1024]{2,1,0:T(8,128)(2,1)} copy(bf16[1,384,1024]{2,1,0:T(8,128)(2,1)} %get-tuple-element.4) | data formatting | bytes 1572864
  161.3 1.2 copy.9
where the time goes:
time: 163 us
  Pallas kernels  157 us (96%)
  local copies, waits for them, and re-layouts  4.8 us (3%)
    pallas_call x1, Pallas kernels, local(): pl.pallas_call(functools.partial(kernel, stages, peers, granules), out_sh...  157 us
    unnamed x3, local copies, waits for them, and re-layouts  4.8 us

commit v1 on v0

v1 whole, which is shorter than its diff:
```python
import functools

import jax
import jax.numpy as jnp
from jax import lax
from jax.experimental import pallas as pl
from jax.experimental.pallas import tpu as pltpu
from jax.sharding import PartitionSpec as P

EPSILON = 1e-06
REACH = (0, 2, -2, 1, -1)
MESH = pl.DeviceIdType.MESH
UNIT = 16
BLOCK = 48


def block_of(rows):
    for block in range(BLOCK, 0, -UNIT):
        if rows % block == 0:
            return block
    return rows


def chip_at(step, z, n):
    low = jnp.where(step <= n - 1 - z, z + step, n - 1 - step)
    high = jnp.where(step <= z, z - step, step)
    return jnp.where(2 * z < n, low, high)


def kernel(
    stages, peers, block,
    env_in, bits_in, tensor_in, env_out, log_out,
    weights, pieces, product, outgoing, peak, peak_sent, peak_all, scale_in, scale_sent,
    load_sem, weight_sem, arrive_sem, line_sem, cross_sem, next_sem,
    peak_send_sem, peak_recv_sem, scale_send_sem, scale_recv_sem, env_sem, first_sem, env_all,
):
    rows, width = outgoing.shape
    granules = rows // block
    n = peers // 2
    stage = lax.axis_index("segment")
    me = lax.axis_index("col")
    z = me // 2
    core = me % 2

    def there(segment, col):
        return {"segment": segment, "col": col}

    load = pltpu.make_async_copy(env_in, env_all, load_sem.at[0])
    keep = pltpu.make_async_copy(env_in, pieces.at[me], load_sem.at[1])
    load.start()

    @pl.when(stage == 0)
    def _():
        keep.start()

    def owner_at(step):
        return chip_at(step // 2, z, n) * 2 + (core + step) % 2

    def weight_copy(owner):
        return pltpu.make_async_copy(
            tensor_in.at[0, :, pl.ds(pl.multiple_of(owner * width, width), width), :],
            weights.at[owner],
            weight_sem.at[owner],
        )

    def start_weight(step, carry):
        weight_copy(owner_at(step)).start()
        return carry

    lax.fori_loop(0, peers, start_weight, 0)

    barrier = pltpu.get_barrier_semaphore()

    def greet(by, carry):
        pl.semaphore_signal(
            barrier, inc=1, device_id=there(stage, (me + by) % peers), device_id_type=MESH
        )
        return carry

    lax.fori_loop(1, peers, greet, 0)

    def meet(turn, carry):
        segment = (stage + 1 + turn // n) % stages
        col = (z + turn) % n * 2 + core
        pl.semaphore_signal(barrier, inc=1, device_id=there(segment, col), device_id_type=MESH)
        return carry

    lax.fori_loop(0, (stages - 1) * n, meet, 0)
    pl.semaphore_wait(barrier, peers - 1 + (stages - 1) * n)

    load.wait()

    @pl.when(stage == 0)
    def _():
        keep.wait()

    def rows_of(granule):
        return pl.ds(pl.multiple_of(granule * block, block), block)

    def send(source, granule, owner, sem, segment, col):
        return pltpu.make_async_remote_copy(
            src_ref=source,
            dst_ref=pieces.at[owner, rows_of(granule), :],
            send_sem=sem,
            recv_sem=arrive_sem.at[granule, owner],
            device_id=there(segment, col),
            device_id_type=MESH,
        )

    def piece(granule, owner):
        return pieces.at[owner, rows_of(granule), :]

    def cross(granule, owner):
        sem = cross_sem.at[granule, owner // 2]
        return send(piece(granule, owner), granule, owner, sem, stage, 2 * z + 1 - core)

    end = (z == 0) | (z == n - 1)

    def spread(act, source, granule, segment, sems, slots):
        for slot in slots:
            by = REACH[slot]
            goes = (z + by >= 0) & (z + by < n)
            if by in (-1, 1):
                goes = goes & jnp.logical_not(end)

            @pl.when(goes)
            def _():
                act(send(source, granule, me, sems.at[slot, granule], segment, me + 2 * by))

    def supply_first(act):
        def supply_chip(by, carry):
            chip = (z + by) % n
            near = jnp.abs(chip - z) == 1

            @pl.when(stage == jnp.where(near, 0, 1))
            def _():
                source = env_all.at[rows_of(0), :]
                act(send(source, 0, me, first_sem.at[by], 0, chip * 2 + core))

            return carry

        lax.fori_loop(1, n, supply_chip, 0)

    def supply(act, granule):
        @pl.when(stage == jnp.minimum(granule + 1, stages - 1))
        def _():
            source = env_all.at[rows_of(granule), :]
            spread(act, source, granule, 0, env_sem, range(1, len(REACH)))

    def onward(act, granule):
        @pl.when(stage < stages - 1)
        def _():
            source = outgoing.at[rows_of(granule), :]
            spread(act, source, granule, stage + 1, next_sem, range(len(REACH)))

    def relays(granule, chip):
        needed = (stage > 0) | (granule > 0)
        return needed & (z != chip) & ((z - chip) % 2 == 0)

    def along(act, granule, chip):
        owner = chip * 2 + core
        source = piece(granule, owner)
        for slot, by in enumerate((1, -1, 2, -2)):
            goes = relays(granule, chip) & ((chip < z) if by > 0 else (chip > z))
            if by in (-1, 1):
                goes = goes | (((stage > 0) | (granule > 0)) & end & (chip == z))

            @pl.when(goes & (z + by >= 0) & (z + by < n))
            def _():
                sem = line_sem.at[slot, granule, chip]
                act(send(source, granule, owner, sem, stage, me + 2 * by))

    def start(copy):
        copy.start()

    def sent(copy):
        copy.wait_send()

    def open_granule(granule):
        @pl.when(stage > 0)
        def _():
            cross(granule, me).wait_recv()

        along(start, granule, z)
        cross(granule, me).start()

    def supply_one(granule, carry):
        supply(start, granule)
        return carry

    supply_first(start)
    lax.fori_loop(1, granules, supply_one, 0)
    chips = [chip_at(step, z, n) for step in range(n)]

    open_granule(0)

    def one_granule(granule, carry):
        here = rows_of(granule)
        bit = bits_in[here, :] == 1

        def take(chip):
            cross(granule, chip * 2 + core).wait_recv()
            along(start, granule, chip)
            cross(granule, chip * 2 + core).start()

        def add(owners, first=False):
            @pl.when(granule == 0)
            def _():
                for owner in owners:
                    weight_copy(owner).wait()

            def against(which):
                total = None
                for owner in owners:
                    one = jnp.dot(
                        piece(granule, owner)[...],
                        weights[owner, which],
                        preferred_element_type=jnp.float32,
                    )
                    total = one if total is None else total + one
                return total

            part = jnp.where(bit, against(1), against(0))
            if first:
                product[here, :] = part
            else:
                product[here, :] += part

        def others(step):
            other = chips[step] * 2 + 1 - core
            cross(granule, other).wait_recv()
            return other

        for step, chip in enumerate(chips):
            own = chip * 2 + core
            last = step == n - 1
            if last:

                @pl.when(granule + 1 < granules)
                def _():
                    open_granule(granule + 1)

            if step > 0:

                @pl.when(relays(granule, chip))
                def _():
                    take(chip)

                if last:
                    add([others(step - 1)])

                @pl.when(jnp.logical_not(relays(granule, chip)))
                def _():
                    take(chip)

            if step == 0 or last:
                add([own], first=step == 0)
            else:
                add([others(step - 1), own])
        add([others(n - 1)])

        done = product[here, :]
        outgoing[here, :] = done.astype(jnp.bfloat16)
        onward(start, granule)
        largest = jnp.max(jnp.abs(done), axis=1, keepdims=True)
        peak[here, :] = jnp.broadcast_to(largest, (block, peak.shape[1]))
        return carry

    lax.fori_loop(0, granules, one_granule, 0)

    mine = jnp.transpose(peak[...])[:8]
    peak_sent[...] = mine

    def peak_copy(by):
        return pltpu.make_async_remote_copy(
            src_ref=peak_sent,
            dst_ref=peak_all.at[by],
            send_sem=peak_send_sem.at[by],
            recv_sem=peak_recv_sem.at[by],
            device_id=there(stage, (me + by) % peers),
            device_id_type=MESH,
        )

    def start_peak(by, carry):
        peak_copy(by).start()
        return carry

    lax.fori_loop(1, peers, start_peak, 0)

    def drain(granule, carry):
        def drain_chip(chip, carry):
            along(sent, granule, chip)
            cross(granule, chip * 2 + core).wait_send()
            return carry

        lax.fori_loop(0, n, drain_chip, 0)
        onward(sent, granule)
        return carry

    lax.fori_loop(0, granules, drain, 0)

    def supplied(granule, carry):
        supply(sent, granule)
        return carry

    supply_first(sent)
    lax.fori_loop(1, granules, supplied, 0)

    scale_copy = pltpu.make_async_remote_copy(
        src_ref=scale_sent,
        dst_ref=scale_in,
        send_sem=scale_send_sem,
        recv_sem=scale_recv_sem,
        device_id=there(stage + 1, me),
        device_id_type=MESH,
    )

    @pl.when(stage == 0)
    def _():
        scale_in[...] = jnp.ones_like(scale_in)

    @pl.when(stage > 0)
    def _():
        scale_copy.wait_recv()

    def take_peak(by, largest):
        peak_copy(by).wait_recv()
        return jnp.maximum(largest, peak_all[by])

    largest = lax.fori_loop(1, peers, take_peak, mine)
    before = scale_in[...]
    scale = largest + EPSILON * before
    scale_sent[...] = scale

    @pl.when(stage < stages - 1)
    def _():
        scale_copy.start()

    log_out[...] = jnp.log(largest / before + EPSILON)[:1]
    by_row = jnp.transpose(jnp.broadcast_to(scale[:1], (128, rows)))[:, :1]
    env_out[0] = (product[...] / by_row).astype(jnp.bfloat16)

    def drain_peak(by, carry):
        peak_copy(by).wait_send()
        return carry

    lax.fori_loop(1, peers, drain_peak, 0)

    @pl.when(stage < stages - 1)
    def _():
        scale_copy.wait_send()


def solution(mesh):
    stages, peers = mesh.shape["segment"], mesh.shape["col"]
    n = peers // 2

    def local(left_env, bit_strings, site_tensors):
        rows, width = left_env.shape
        block = block_of(rows)
        granules = rows // block
        vmem = pl.BlockSpec(memory_space=pltpu.VMEM)
        anywhere = pl.BlockSpec(memory_space=pl.ANY)
        dma = pltpu.SemaphoreType.DMA
        return pl.pallas_call(
            functools.partial(kernel, stages, peers, block),
            out_shape=(
                jax.ShapeDtypeStruct((1, rows, width), jnp.bfloat16),
                jax.ShapeDtypeStruct((1, rows), jnp.float32),
            ),
            in_specs=[anywhere, vmem, anywhere],
            out_specs=(vmem, vmem),
            scratch_shapes=[
                pltpu.VMEM((peers, 2, width, width), jnp.bfloat16),
                pltpu.VMEM((peers, rows, width), jnp.bfloat16),
                pltpu.VMEM((rows, width), jnp.float32),
                pltpu.VMEM((rows, width), jnp.bfloat16),
                pltpu.VMEM((rows, 128), jnp.float32),
                pltpu.VMEM((8, rows), jnp.float32),
                pltpu.VMEM((peers, 8, rows), jnp.float32),
                pltpu.VMEM((8, rows), jnp.float32),
                pltpu.VMEM((8, rows), jnp.float32),
                dma((2,)),
                dma((peers,)),
                dma((granules, peers)),
                dma((4, granules, n)),
                dma((granules, n)),
                dma((5, granules)),
                dma((peers,)),
                dma((peers,)),
                dma,
                dma,
                dma((5, granules)),
                dma((n,)),
                pltpu.VMEM((rows, width), jnp.bfloat16),
            ],
            compiler_params=pltpu.CompilerParams(
                collective_id=0, has_side_effects=True, vmem_limit_bytes=60 * 1024 * 1024
            ),
        )(left_env, bit_strings, site_tensors)

    return jax.shard_map(
        local,
        mesh=mesh,
        in_specs=(P(None, "col"), P(None, "segment"), P("segment", None, None, "col")),
        out_specs=(P("segment", None, "col"), P("segment", None)),
        check_vma=False,
    )
```

time: 163 us -> 142 us (0.87)
  Pallas kernels: 157 us -> 136 us
    pallas_call x1, Pallas kernels: 157 us -> 136 us  [local(): pl.pallas_call(functools.partial(kernel, stages, peers, block), out_shape...]
where the time goes in v1:
time: 142 us; the launch traced here: 141 us
  Pallas kernels  136 us (96%)
  local copies, waits for them, and re-layouts  4.8 us (3%)
    pallas_call x1, Pallas kernels, local(): pl.pallas_call(functools.partial(kernel, stages, peers, block), out_shape...  136 us
    unnamed x3, local copies, waits for them, and re-layouts  4.8 us

profile of v1, /device:TPU:7, one launch (start us, length us, event | category | flops | bytes accessed | tf_op | source)
XLA Modules:
  0.0 141.5 jit_solution(1643760062828146533)
XLA Ops:
  0.6 1.5 %copy.5.bits_in = s32[384,1]{1,0:T(8,128)} copy(s32[384,1]{0,1:T(1,128)} %param.4) | data formatting | bytes 3072 | tf_op args[1]
  2.1 136.0 %shard_map.50 = (bf16[1,384,1024]{2,1,0:T(8,128)(2,1)}, f32[1,384]{1,0:T(1,128)}) custom-call(bf16[384,1024]{1,0:T(8,128)(2,1)} %env_in.1, s32[384,1]{1,0:T(8,128)} %copy.5.bits_in, bf16[1,2,8192,1024]{3,2,1,0:T(8,128)(2,1)} %tensor_in.1), custom_call_target="tpu_custom_call" | custom-call | tf_op jit(solution)/shard_map/pallas_call | solution.py:365
  138.2 2.1 %copy.8 = bf16[1,384,1024]{2,1,0:T(8,128)(2,1)} copy(bf16[1,384,1024]{2,1,0:T(8,128)(2,1)} %get-tuple-element.4) | data formatting | bytes 1572864
  140.2 1.2 copy.9
